TPU v7x, 256 devices: a whole 4x4x8 slice. The times are simulated.
256 devices in a mesh: dp: 32 (over y, z), vocab: 8 (over x, core).
Axes of the slice: x: 4, y: 4, z: 8, core: 2. Of those that a mesh axis runs over, the one named last changes fastest.
Arguments:
- hidden: bfloat16 [24576, 2048], P('dp', 'vocab')
- gain: bfloat16 [2048], replicated, may hold values from 0.5 to 1.5
- head: bfloat16 [2048, 32000], P('dp', 'vocab')
- target_ids: int32 [24576], P('dp'), may hold values from 0 to 31999
- seq_lens: int32 [64], replicated, may hold values from 64 to 704, as said below
- seq_owner: int32 [64], replicated, may hold values from 0 to 31, as said below
Outputs:
- logprob: float32 [24576], P('dp')
- entropy: float32 [24576], P('dp')
Inputs may be any that keep to these rules, and one draw needn't show every extreme that they name: `seq_lens`: the lengths of the sequences owned by one dp index sum to at most 768; in every draw the sequences of some dp index sum to exactly 768. `seq_owner`: every dp index owns exactly 2 sequences.
All inputs are finite; a program needn't handle non-finite values.
Results may differ from a plain program's by a relative error of at most 0.0075.
Values may be sent and summed in bfloat16 or wider, within the bound.
A program may use at most 64 MiB of HBM per device.

v0:
```python
import jax
import jax.numpy as jnp
from jax import lax
from jax.sharding import PartitionSpec as P

EPS = 1e-05


def row_stats(normed, token_ids, columns, offset):
    count = normed.shape[0]
    width = normed.shape[1]
    block_rows = min(128, count)
    blocks = count // block_rows
    breadth = columns.shape[1]

    def compute(block_norm, block_ids):
        logits = jnp.dot(block_norm, columns, preferred_element_type=jnp.float32)
        top = jnp.max(logits, axis=1)
        expo = jnp.exp(logits - top[:, None])
        total = jnp.sum(expo, axis=1)
        weighted = jnp.sum(expo * logits, axis=1)
        local_id = block_ids - offset
        matches = jnp.arange(breadth, dtype=jnp.int32)[None, :] == local_id[:, None]
        picked = jnp.sum(jnp.where(matches, logits, 0.0), axis=1)
        return (top, total, weighted, picked)

    def per_block(item):
        block_norm, block_ids, start = item
        return compute(block_norm, block_ids)

    starts = jnp.arange(blocks, dtype=jnp.int32) * block_rows
    result = lax.map(
        per_block,
        (normed.reshape(blocks, block_rows, width), token_ids.reshape(blocks, block_rows), starts),
    )
    return tuple((member.reshape(count) for member in result))


def local(hidden, gain, head, target_ids, seq_lens, seq_owner):
    groups = lax.axis_size("dp")
    position = lax.axis_index("dp")
    slice_index = lax.axis_index("vocab")
    slots = hidden.shape[0]
    breadth = head.shape[1]
    owners = jnp.arange(groups, dtype=jnp.int32)
    loads = jnp.sum(jnp.where(seq_owner[:, None] == owners[None, :], seq_lens[:, None], 0), axis=0)
    own_live = jnp.arange(slots, dtype=jnp.int32) < loads[position]
    features = lax.all_gather(hidden, "vocab", axis=1, tiled=True)
    wide = features.astype(jnp.float32)
    normed = (
        wide
        * lax.rsqrt(jnp.mean(wide * wide, axis=1, keepdims=True) + EPS)
        * gain.astype(jnp.float32)
    ).astype(jnp.bfloat16)
    columns = lax.all_gather(head, "dp", axis=0, tiled=True)
    stats = row_stats(normed, target_ids, columns, slice_index * breadth)
    top = lax.pmax(stats[0], "vocab")
    factor = jnp.exp(stats[0] - top)
    total, weighted, picked = lax.psum((stats[1] * factor, stats[2] * factor, stats[3]), "vocab")
    lse = top + jnp.log(total)
    logprob = picked - lse
    entropy = lse - weighted / total
    return (jnp.where(own_live, logprob, 0.0), jnp.where(own_live, entropy, 0.0))


def solution(mesh):
    return jax.shard_map(
        local,
        mesh=mesh,
        in_specs=(P("dp", "vocab"), P(), P("dp", "vocab"), P("dp"), P(), P()),
        out_specs=(P("dp"), P("dp")),
        check_vma=False,
    )
```

profile of v0, /device:TPU:8, one launch (start us, length us, event | category | flops | bytes accessed | tf_op | source)
XLA Modules:
  0.0 306.3 jit_solution(14415921997200401669)
XLA Ops:
  7.2 0.7 all-gather.3.cloned.1.call-update
  7.9 0.7 all-gather.5.cloned.1.call-update
  8.7 0.7 convert_element_type.10
  9.4 0.8 select_reduce_fusion.1
  10.2 0.6 dynamic_slice.11
  10.8 36.1 %all-gather.3.cloned.1.call-done = bf16[768,2048]{1,0:T(8,128)(2,1)} async-done(((bf16[768,256]{1,0:T(8,128)(2,1)}), bf16[768,2048]{1,0:T(8,128)(2,1)}) %all-gather.3.cloned.1.call-update) | async-done | bytes 3145744 | tf_op jit(solution)/shard_map/all_gather | solution.py:48
  46.9 2.7 fusion.5
  49.6 0.1 copy-done
  49.7 2.5 fusion.7
  52.2 137.7 %all-gather.5.cloned.1.call-done = bf16[2048,4000]{1,0:T(8,128)(2,1)} async-done(((bf16[64,4000]{1,0:T(8,128)(2,1)}), bf16[2048,4000]{1,0:T(8,128)(2,1)}) %all-gather.5.cloned.1.call-update) | async-done | bytes 16384016 | tf_op jit(solution)/shard_map/all_gather | solution.py:55
  189.9 70.6 %while.16 = (s32[]{:T(128)}, f32[6,128]{1,0:T(8,128)S(1)}, f32[6,128]{1,0:T(8,128)S(1)}, f32[6,128]{1,0:T(8,128)S(1)}, f32[6,128]{1,0:T(8,128)S(1)}, /*index=5*/...) while((s32[]{:T(128)}, f32[6,128]{1,0:T(8,128)S(1)}, ...), condition=%wide.region_7.8_spmd, body=%wide.region_2.7_spmd.sunk | while | flops 2101247616 | bytes 21406340 | solution.py:32
  189.9 10.2 %fusion.13 = (f32[128]{0:T(128)S(1)}, f32[128,4000]{0,1:T(8,128)S(1)}) fusion(bf16[2048,4000]{1,0:T(8,128)(2,1)} %get-tuple-element.179, bf16[6,128,2048]{2,1,0:T(8,128)(2,1)} %get-tuple-element.178, s32[]{:T(128)} %get-tuple-element.162), kind=kOutput, calls=%fused_computation.25.clone.1 | convolution fusion | flops 2097663872 | bytes 19350528 | tf_op jit(solution)/shard_map/while/body/eval_jaxpr/dot_general | solution.py:17
  200.1 0.7 subtract_bitcast_fusion.2
  200.8 0.7 multiply_reduce_fusion.2
  201.6 10.2 %fusion.13 = (f32[128]{0:T(128)S(1)}, f32[128,4000]{0,1:T(8,128)S(1)}) fusion(bf16[2048,4000]{1,0:T(8,128)(2,1)} %get-tuple-element.179, bf16[6,128,2048]{2,1,0:T(8,128)(2,1)} %get-tuple-element.178, s32[]{:T(128)} %get-tuple-element.162), kind=kOutput, calls=%fused_computation.25.clone.1 | convolution fusion | flops 2097663872 | bytes 19350528 | tf_op jit(solution)/shard_map/while/body/eval_jaxpr/dot_general | solution.py:17
  211.9 0.7 subtract_bitcast_fusion.2
  212.6 0.7 multiply_reduce_fusion.2
  213.4 10.2 %fusion.13 = (f32[128]{0:T(128)S(1)}, f32[128,4000]{0,1:T(8,128)S(1)}) fusion(bf16[2048,4000]{1,0:T(8,128)(2,1)} %get-tuple-element.179, bf16[6,128,2048]{2,1,0:T(8,128)(2,1)} %get-tuple-element.178, s32[]{:T(128)} %get-tuple-element.162), kind=kOutput, calls=%fused_computation.25.clone.1 | convolution fusion | flops 2097663872 | bytes 19350528 | tf_op jit(solution)/shard_map/while/body/eval_jaxpr/dot_general | solution.py:17
  223.7 0.7 subtract_bitcast_fusion.2
  224.4 0.7 multiply_reduce_fusion.2
  225.2 10.2 %fusion.13 = (f32[128]{0:T(128)S(1)}, f32[128,4000]{0,1:T(8,128)S(1)}) fusion(bf16[2048,4000]{1,0:T(8,128)(2,1)} %get-tuple-element.179, bf16[6,128,2048]{2,1,0:T(8,128)(2,1)} %get-tuple-element.178, s32[]{:T(128)} %get-tuple-element.162), kind=kOutput, calls=%fused_computation.25.clone.1 | convolution fusion | flops 2097663872 | bytes 19350528 | tf_op jit(solution)/shard_map/while/body/eval_jaxpr/dot_general | solution.py:17
  235.4 0.7 subtract_bitcast_fusion.2
  236.1 0.7 multiply_reduce_fusion.2
  237.0 10.2 %fusion.13 = (f32[128]{0:T(128)S(1)}, f32[128,4000]{0,1:T(8,128)S(1)}) fusion(bf16[2048,4000]{1,0:T(8,128)(2,1)} %get-tuple-element.179, bf16[6,128,2048]{2,1,0:T(8,128)(2,1)} %get-tuple-element.178, s32[]{:T(128)} %get-tuple-element.162), kind=kOutput, calls=%fused_computation.25.clone.1 | convolution fusion | flops 2097663872 | bytes 19350528 | tf_op jit(solution)/shard_map/while/body/eval_jaxpr/dot_general | solution.py:17
  247.2 0.7 subtract_bitcast_fusion.2
  247.9 0.7 multiply_reduce_fusion.2
  248.7 10.2 %fusion.13 = (f32[128]{0:T(128)S(1)}, f32[128,4000]{0,1:T(8,128)S(1)}) fusion(bf16[2048,4000]{1,0:T(8,128)(2,1)} %get-tuple-element.179, bf16[6,128,2048]{2,1,0:T(8,128)(2,1)} %get-tuple-element.178, s32[]{:T(128)} %get-tuple-element.162), kind=kOutput, calls=%fused_computation.25.clone.1 | convolution fusion | flops 2097663872 | bytes 19350528 | tf_op jit(solution)/shard_map/while/body/eval_jaxpr/dot_general | solution.py:17
  259.0 0.7 subtract_bitcast_fusion.2
  259.7 0.7 multiply_reduce_fusion.2
  260.5 14.1 %pmax.7 = f32[768]{0:T(1024)S(1)} all-reduce(f32[768]{0:T(1024)S(1)} %bitcast.42), channel_id=1, replica_groups=mesh['dp'=32,'vocab'=8] {'vocab'}, use_global_device_ids=true, to_apply=%region_9.10 | all-reduce | flops 768 | bytes 6144 | tf_op jit(solution)/shard_map/pmax | solution.py:57
  274.7 23.6 %all-reduce = (f32[768]{0:T(1024)S(1)}, f32[768]{0:T(1024)S(1)}, f32[768]{0:T(1024)S(1)}) all-reduce(f32[768]{0:T(1024)S(1)} %bitcast.43, f32[768]{0:T(1024)S(1)} %get-tuple-element.85, f32[768]{0:T(1024)S(1)} %get-tuple-element.84), channel_id=1, replica_groups=mesh['dp'=32,'vocab'=8] {'vocab'}, use_global_device_ids=true, to_apply=%region_8.9 | all-reduce | flops 2304 | bytes 18432 | tf_op jit(solution)/shard_map/psum | solution.py:59
  298.2 1.2 subtract_select_fusion
  (33 shorter events, 0.9 us)
Async XLA Ops:
  7.2 39.7 %all-gather.3.cloned.1.call-start = ((), (), s32[]{:S(2)}) async-start(), calls=%async_computation | async-start | bytes 3538944 | tf_op jit(solution)/shard_map/all_gather | solution.py:48
  7.9 182.0 %all-gather.5.cloned.1.call-start = ((), (), s32[]{:S(2)}) async-start(), calls=%async_computation.1 | async-start | bytes 17301504 | tf_op jit(solution)/shard_map/all_gather | solution.py:55
  46.9 2.8 copy-start
Sparse Core Ops, SparseCore 0:
  9.8 37.0 all-gather.2
  49.5 140.3 all-gather.4
where the time goes:
time: 307 us; the launch traced here: 306 us
  waiting for transfers between devices  175 us (57%)
  matrix products  61.4 us (20%)
  blocking collectives  37.7 us (12%)
  other arithmetic  16.2 us (5%)
  between operations  14.1 us (5%)
    all_gather x1, waiting for transfers between devices, local(): columns = lax.all_gather(head, 'dp', axis=0, tiled=True)  138 us
    dot_general x6, matrix products, compute(): logits = jnp.dot(block_norm, columns, preferred_element_type=jnp.float32)  61.4 us
    all_gather x1, waiting for transfers between devices, local(): features = lax.all_gather(hidden, 'vocab', axis=1, tiled=True)  36.1 us
    psum x1, blocking collectives, local(): lax.psum((stats[1] * factor, stats[2] * factor, stats[3]), 'vocab')  23.6 us
    pmax x1, blocking collectives, local(): top = lax.pmax(stats[0], 'vocab')  14.1 us
  transfers between devices with their start and end apart: 2, of which 2 were waited for; matrix products, arithmetic and copies ran while one was open for 2% of the time, Pallas kernels for 0%

commit v1 on v0

--- a/solution.py
+++ b/solution.py
@@ -45,7 +45,14 @@
     owners = jnp.arange(groups, dtype=jnp.int32)
     loads = jnp.sum(jnp.where(seq_owner[:, None] == owners[None, :], seq_lens[:, None], 0), axis=0)
     own_live = jnp.arange(slots, dtype=jnp.int32) < loads[position]
-    features = lax.all_gather(hidden, "vocab", axis=1, tiled=True)
+    ring = [hidden]
+    for hop in range(7):
+        ring.append(lax.ppermute(ring[-1], "vocab", [(dev, (dev + 1) % 8) for dev in range(8)]))
+    features = jnp.roll(
+        jnp.concatenate(ring[::-1], axis=1),
+        (lax.axis_index("vocab") + 1) * ring[0].shape[1],
+        axis=1,
+    )
     wide = features.astype(jnp.float32)
     normed = (
         wide

time: 307 us -> 270 us (0.88)
  waiting for transfers between devices: 175 us -> 139 us
    ppermute x0 -> x7, waiting for transfers between devices: none -> 57 us  [local(): lax.ppermute(ring[-1], 'vocab', [(dev, (dev + 1) % 8) for dev in range(8)])]
    all_gather x1, waiting for transfers between devices: 138 us -> 81.8 us  [local(): columns = lax.all_gather(head, 'dp', axis=0, tiled=True)]
    all_gather x1 -> x0, waiting for transfers between devices: 36.1 us -> none  [local(): features = lax.all_gather(hidden, 'vocab', axis=1, tiled=True)]
  transfers between devices with their start and end apart: 2 -> 8, of which waited for: 2 -> 8; matrix products, arithmetic and copies ran while one was open for 2% -> 2% of each run, Pallas kernels for 0% -> 0%
where the time goes in v1:
time: 270 us; the launch traced here: 269 us
  waiting for transfers between devices  139 us (51%)
  matrix products  61.4 us (23%)
  blocking collectives  37.7 us (14%)
  other arithmetic  14.2 us (5%)
  between operations  14.2 us (5%)
    all_gather x1, waiting for transfers between devices, local(): columns = lax.all_gather(head, 'dp', axis=0, tiled=True)  81.8 us
    dot_general x6, matrix products, compute(): logits = jnp.dot(block_norm, columns, preferred_element_type=jnp.float32)  61.4 us
    ppermute x7, waiting for transfers between devices, local(): lax.ppermute(ring[-1], 'vocab', [(dev, (dev + 1) % 8) for dev in range(8)])  57 us
    psum x1, blocking collectives, local(): lax.psum((stats[1] * factor, stats[2] * factor, stats[3]), 'vocab')  23.6 us
    pmax x1, blocking collectives, local(): top = lax.pmax(stats[0], 'vocab')  14.1 us
  transfers between devices with their start and end apart: 8, of which 8 were waited for; matrix products, arithmetic and copies ran while one was open for 2% of the time, Pallas kernels for 0%

profile of v1, /device:TPU:8, one launch (start us, length us, event | category | flops | bytes accessed | tf_op | source)
XLA Modules:
  0.0 269.2 jit_solution(11210723892366828981)
XLA Ops:
  7.9 8.6 %collective-permute-done = bf16[768,256]{1,0:T(8,128)(2,1)S(1)} collective-permute-done((bf16[768,256]{1,0:T(8,128)(2,1)}, bf16[768,256]{1,0:T(8,128)(2,1)S(1)}, u32[]{:S(2)}, u32[]{:S(2)}) %collective-permute-start) | collective-permute-done | bytes 393248 | tf_op jit(solution)/shard_map/ppermute | solution.py:50
  16.5 8.4 %collective-permute-done.1 = bf16[768,256]{1,0:T(8,128)(2,1)S(1)} collective-permute-done((bf16[768,256]{1,0:T(8,128)(2,1)S(1)}, bf16[768,256]{1,0:T(8,128)(2,1)S(1)}, u32[]{:S(2)}, u32[]{:S(2)}) %collective-permute-start.1) | collective-permute-done | bytes 393248 | tf_op jit(solution)/shard_map/ppermute | solution.py:50
  25.0 8.4 %collective-permute-done.2 = bf16[768,256]{1,0:T(8,128)(2,1)S(1)} collective-permute-done((bf16[768,256]{1,0:T(8,128)(2,1)S(1)}, bf16[768,256]{1,0:T(8,128)(2,1)S(1)}, u32[]{:S(2)}, u32[]{:S(2)}) %collective-permute-start.2) | collective-permute-done | bytes 393248 | tf_op jit(solution)/shard_map/ppermute | solution.py:50
  33.4 8.4 %collective-permute-done.3 = bf16[768,256]{1,0:T(8,128)(2,1)S(1)} collective-permute-done((bf16[768,256]{1,0:T(8,128)(2,1)S(1)}, bf16[768,256]{1,0:T(8,128)(2,1)S(1)}, u32[]{:S(2)}, u32[]{:S(2)}) %collective-permute-start.3) | collective-permute-done | bytes 393248 | tf_op jit(solution)/shard_map/ppermute | solution.py:50
  41.8 8.4 %collective-permute-done.4 = bf16[768,256]{1,0:T(8,128)(2,1)S(1)} collective-permute-done((bf16[768,256]{1,0:T(8,128)(2,1)S(1)}, bf16[768,256]{1,0:T(8,128)(2,1)S(1)}, u32[]{:S(2)}, u32[]{:S(2)}) %collective-permute-start.4) | collective-permute-done | bytes 393248 | tf_op jit(solution)/shard_map/ppermute | solution.py:50
  50.2 8.4 %collective-permute-done.5 = bf16[768,256]{1,0:T(8,128)(2,1)S(1)} collective-permute-done((bf16[768,256]{1,0:T(8,128)(2,1)S(1)}, bf16[768,256]{1,0:T(8,128)(2,1)S(1)}, u32[]{:S(2)}, u32[]{:S(2)}) %collective-permute-start.5) | collective-permute-done | bytes 393248 | tf_op jit(solution)/shard_map/ppermute | solution.py:50
  58.6 0.7 convert_element_type.10
  59.3 0.8 select_reduce_fusion.1
  60.7 6.3 %collective-permute-done.6 = bf16[768,256]{1,0:T(8,128)(2,1)S(1)} collective-permute-done((bf16[768,256]{1,0:T(8,128)(2,1)S(1)}, bf16[768,256]{1,0:T(8,128)(2,1)S(1)}, u32[]{:S(2)}, u32[]{:S(2)}) %collective-permute-start.6) | collective-permute-done | bytes 393248 | tf_op jit(solution)/shard_map/ppermute | solution.py:50
  67.9 0.7 fusion.5
  68.6 2.5 fusion.7
  71.1 81.8 %all-gather.2.cloned.1.call-done = bf16[2048,4000]{1,0:T(8,128)(2,1)} async-done(((bf16[64,4000]{1,0:T(8,128)(2,1)}), bf16[2048,4000]{1,0:T(8,128)(2,1)}) %all-gather.2.cloned.1.call-update) | async-done | bytes 16384016 | tf_op jit(solution)/shard_map/all_gather | solution.py:62
  152.8 70.6 %while.16 = (s32[]{:T(128)}, f32[6,128]{1,0:T(8,128)S(1)}, f32[6,128]{1,0:T(8,128)S(1)}, f32[6,128]{1,0:T(8,128)S(1)}, f32[6,128]{1,0:T(8,128)S(1)}, /*index=5*/...) while((s32[]{:T(128)}, f32[6,128]{1,0:T(8,128)S(1)}, ...), condition=%wide.region_7.8_spmd, body=%wide.region_2.7_spmd.sunk | while | flops 2101247616 | bytes 21406340 | solution.py:32
  152.8 10.2 %fusion.13 = (f32[128]{0:T(128)S(1)}, f32[128,4000]{0,1:T(8,128)S(1)}) fusion(bf16[2048,4000]{1,0:T(8,128)(2,1)} %get-tuple-element.179, bf16[6,128,2048]{2,1,0:T(8,128)(2,1)} %get-tuple-element.178, s32[]{:T(128)} %get-tuple-element.162), kind=kOutput, calls=%fused_computation.41.clone.1 | convolution fusion | flops 2097663872 | bytes 19350528 | tf_op jit(solution)/shard_map/while/body/eval_jaxpr/dot_general | solution.py:17
  163.1 0.7 subtract_bitcast_fusion.2
  163.8 0.7 multiply_reduce_fusion.2
  164.6 10.2 %fusion.13 = (f32[128]{0:T(128)S(1)}, f32[128,4000]{0,1:T(8,128)S(1)}) fusion(bf16[2048,4000]{1,0:T(8,128)(2,1)} %get-tuple-element.179, bf16[6,128,2048]{2,1,0:T(8,128)(2,1)} %get-tuple-element.178, s32[]{:T(128)} %get-tuple-element.162), kind=kOutput, calls=%fused_computation.41.clone.1 | convolution fusion | flops 2097663872 | bytes 19350528 | tf_op jit(solution)/shard_map/while/body/eval_jaxpr/dot_general | solution.py:17
  174.8 0.7 subtract_bitcast_fusion.2
  175.5 0.7 multiply_reduce_fusion.2
  176.4 10.2 %fusion.13 = (f32[128]{0:T(128)S(1)}, f32[128,4000]{0,1:T(8,128)S(1)}) fusion(bf16[2048,4000]{1,0:T(8,128)(2,1)} %get-tuple-element.179, bf16[6,128,2048]{2,1,0:T(8,128)(2,1)} %get-tuple-element.178, s32[]{:T(128)} %get-tuple-element.162), kind=kOutput, calls=%fused_computation.41.clone.1 | convolution fusion | flops 2097663872 | bytes 19350528 | tf_op jit(solution)/shard_map/while/body/eval_jaxpr/dot_general | solution.py:17
  186.6 0.7 subtract_bitcast_fusion.2
  187.3 0.7 multiply_reduce_fusion.2
  188.1 10.2 %fusion.13 = (f32[128]{0:T(128)S(1)}, f32[128,4000]{0,1:T(8,128)S(1)}) fusion(bf16[2048,4000]{1,0:T(8,128)(2,1)} %get-tuple-element.179, bf16[6,128,2048]{2,1,0:T(8,128)(2,1)} %get-tuple-element.178, s32[]{:T(128)} %get-tuple-element.162), kind=kOutput, calls=%fused_computation.41.clone.1 | convolution fusion | flops 2097663872 | bytes 19350528 | tf_op jit(solution)/shard_map/while/body/eval_jaxpr/dot_general | solution.py:17
  198.4 0.7 subtract_bitcast_fusion.2
  199.9 10.2 %fusion.13 = (f32[128]{0:T(128)S(1)}, f32[128,4000]{0,1:T(8,128)S(1)}) fusion(bf16[2048,4000]{1,0:T(8,128)(2,1)} %get-tuple-element.179, bf16[6,128,2048]{2,1,0:T(8,128)(2,1)} %get-tuple-element.178, s32[]{:T(128)} %get-tuple-element.162), kind=kOutput, calls=%fused_computation.41.clone.1 | convolution fusion | flops 2097663872 | bytes 19350528 | tf_op jit(solution)/shard_map/while/body/eval_jaxpr/dot_general | solution.py:17
  210.2 0.7 subtract_bitcast_fusion.2
  211.7 10.2 %fusion.13 = (f32[128]{0:T(128)S(1)}, f32[128,4000]{0,1:T(8,128)S(1)}) fusion(bf16[2048,4000]{1,0:T(8,128)(2,1)} %get-tuple-element.179, bf16[6,128,2048]{2,1,0:T(8,128)(2,1)} %get-tuple-element.178, s32[]{:T(128)} %get-tuple-element.162), kind=kOutput, calls=%fused_computation.41.clone.1 | convolution fusion | flops 2097663872 | bytes 19350528 | tf_op jit(solution)/shard_map/while/body/eval_jaxpr/dot_general | solution.py:17
  221.9 0.7 subtract_bitcast_fusion.2
  222.6 0.7 multiply_reduce_fusion.2
  223.5 14.1 %pmax.7 = f32[768]{0:T(1024)S(1)} all-reduce(f32[768]{0:T(1024)S(1)} %bitcast.42), channel_id=1, replica_groups=mesh['dp'=32,'vocab'=8] {'vocab'}, use_global_device_ids=true, to_apply=%region_9.10 | all-reduce | flops 768 | bytes 6144 | tf_op jit(solution)/shard_map/pmax | solution.py:64
  237.6 23.6 %all-reduce = (f32[768]{0:T(1024)S(1)}, f32[768]{0:T(1024)S(1)}, f32[768]{0:T(1024)S(1)}) all-reduce(f32[768]{0:T(1024)S(1)} %bitcast.43, f32[768]{0:T(1024)S(1)} %get-tuple-element.85, f32[768]{0:T(1024)S(1)} %get-tuple-element.84), channel_id=1, replica_groups=mesh['dp'=32,'vocab'=8] {'vocab'}, use_global_device_ids=true, to_apply=%region_8.9 | all-reduce | flops 2304 | bytes 18432 | tf_op jit(solution)/shard_map/psum | solution.py:66
  261.2 1.2 subtract_select_fusion
  (60 shorter events, 4.3 us)
Async XLA Ops:
  7.2 60.2 %copy-start = (bf16[768,256]{1,0:T(8,128)(2,1)S(1)}, bf16[768,256]{1,0:T(8,128)(2,1)}, u32[]{:S(2)}) copy-start(bf16[768,256]{1,0:T(8,128)(2,1)} %param.8) | copy-start | bytes 1179652
  7.2 145.7 %all-gather.2.cloned.1.call-start = ((), (), s32[]{:S(2)}) async-start(), calls=%async_computation | async-start | bytes 17301504 | tf_op jit(solution)/shard_map/all_gather | solution.py:62
  7.9 8.6 %collective-permute-start = (bf16[768,256]{1,0:T(8,128)(2,1)}, bf16[768,256]{1,0:T(8,128)(2,1)S(1)}, u32[]{:S(2)}, u32[]{:S(2)}) collective-permute-start(bf16[768,256]{1,0:T(8,128)(2,1)} %param.8), channel_id=1, source_target_pairs={{0,1},{1,2},{2,3},{3,4},{4,5},{5,6},{6,7},{7,0},{8,9},{9,10},{10,1... | collective-permute-start | bytes 1179656 | tf_op jit(solution)/shard_map/ppermute | solution.py:50
  16.5 8.4 %collective-permute-start.1 = (bf16[768,256]{1,0:T(8,128)(2,1)S(1)}, bf16[768,256]{1,0:T(8,128)(2,1)S(1)}, u32[]{:S(2)}, u32[]{:S(2)}) collective-permute-start(bf16[768,256]{1,0:T(8,128)(2,1)S(1)} %collective-permute-done), channel_id=1, source_target_pairs={{0,1},{1,2},{2,3},{3,4},{4,5},{5,6},{6,7},{7,0},{8,9},{9,10},{10,1... | collective-permute-start | bytes 1179656 | tf_op jit(solution)/shard_map/ppermute | solution.py:50
  25.0 8.4 %collective-permute-start.2 = (bf16[768,256]{1,0:T(8,128)(2,1)S(1)}, bf16[768,256]{1,0:T(8,128)(2,1)S(1)}, u32[]{:S(2)}, u32[]{:S(2)}) collective-permute-start(bf16[768,256]{1,0:T(8,128)(2,1)S(1)} %collective-permute-done.1), channel_id=1, source_target_pairs={{0,1},{1,2},{2,3},{3,4},{4,5},{5,6},{6,7},{7,0},{8,9},{9,10},{10,1... | collective-permute-start | bytes 1179656 | tf_op jit(solution)/shard_map/ppermute | solution.py:50
  33.4 8.4 %collective-permute-start.3 = (bf16[768,256]{1,0:T(8,128)(2,1)S(1)}, bf16[768,256]{1,0:T(8,128)(2,1)S(1)}, u32[]{:S(2)}, u32[]{:S(2)}) collective-permute-start(bf16[768,256]{1,0:T(8,128)(2,1)S(1)} %collective-permute-done.2), channel_id=1, source_target_pairs={{0,1},{1,2},{2,3},{3,4},{4,5},{5,6},{6,7},{7,0},{8,9},{9,10},{10,1... | collective-permute-start | bytes 1179656 | tf_op jit(solution)/shard_map/ppermute | solution.py:50
  41.8 8.4 %collective-permute-start.4 = (bf16[768,256]{1,0:T(8,128)(2,1)S(1)}, bf16[768,256]{1,0:T(8,128)(2,1)S(1)}, u32[]{:S(2)}, u32[]{:S(2)}) collective-permute-start(bf16[768,256]{1,0:T(8,128)(2,1)S(1)} %collective-permute-done.3), channel_id=1, source_target_pairs={{0,1},{1,2},{2,3},{3,4},{4,5},{5,6},{6,7},{7,0},{8,9},{9,10},{10,1... | collective-permute-start | bytes 1179656 | tf_op jit(solution)/shard_map/ppermute | solution.py:50
  50.2 8.4 %collective-permute-start.5 = (bf16[768,256]{1,0:T(8,128)(2,1)S(1)}, bf16[768,256]{1,0:T(8,128)(2,1)S(1)}, u32[]{:S(2)}, u32[]{:S(2)}) collective-permute-start(bf16[768,256]{1,0:T(8,128)(2,1)S(1)} %collective-permute-done.4), channel_id=1, source_target_pairs={{0,1},{1,2},{2,3},{3,4},{4,5},{5,6},{6,7},{7,0},{8,9},{9,10},{10,1... | collective-permute-start | bytes 1179656 | tf_op jit(solution)/shard_map/ppermute | solution.py:50
  58.6 8.4 %collective-permute-start.6 = (bf16[768,256]{1,0:T(8,128)(2,1)S(1)}, bf16[768,256]{1,0:T(8,128)(2,1)S(1)}, u32[]{:S(2)}, u32[]{:S(2)}) collective-permute-start(bf16[768,256]{1,0:T(8,128)(2,1)S(1)} %collective-permute-done.5), channel_id=1, source_target_pairs={{0,1},{1,2},{2,3},{3,4},{4,5},{5,6},{6,7},{7,0},{8,9},{9,10},{10,1... | collective-permute-start | bytes 1179656 | tf_op jit(solution)/shard_map/ppermute | solution.py:50
Sparse Core Ops, SparseCore 0:
  10.6 142.1 all-gather.1
